TPU v7x, 256 devices: a whole 4x4x8 slice. The times are simulated.
256 devices in a mesh: elem: 8 (over z), tm: 32 (over y, x, core).
Axes of the slice: x: 4, y: 4, z: 8, core: 2. Of those that a mesh axis runs over, the one named last changes fastest.
Arguments:
- samples: bfloat16 [24576, 2048], P('tm', 'elem'), may hold values from -160 to 160
- taps_weight: bfloat16 [16, 2048, 512], P(None, 'elem'), may hold values from -0.046875 to 0.046875
- retain: float32 [24576], P('tm')
Outputs:
- whitened: float32 [512, 24576], P('elem', 'tm')
All inputs are finite; a program needn't handle non-finite values.
Results may differ from a plain program's by a relative error of at most 0.0003.
Values may be sent and summed in bfloat16 or wider, within the bound.
No kernel may reach another device: no remote copies, remote signals or barrier semaphores. Data moves between devices by JAX's collectives and lax.ppermute only.
A program may use at most 192 MiB of HBM per device.

v0:
```python
import jax
import jax.numpy as jnp
from jax import lax
from jax.sharding import PartitionSpec as P

loading_level = 0.1


def shifted(array, axis, by):
    size = lax.axis_size(axis)
    pairs = [(i, i + by) for i in range(size) if 0 <= i + by < size]
    return lax.ppermute(array, axis, pairs)


def entering(value, axis, join, neutral):
    count, mine = (lax.axis_size(axis), lax.axis_index(axis))
    pieces = jax.tree.map(lambda part: lax.all_gather(part, axis), value)
    so_far = jax.tree.map(
        lambda part, zero: jnp.full_like(part, 0) + jnp.asarray(zero, part.dtype), value, neutral
    )

    def hop(position, so_far):
        longer = join(so_far, jax.tree.map(lambda part: part[position], pieces))
        return jax.tree.map(lambda new, old: jnp.where(position < mine, new, old), longer, so_far)

    return lax.fori_loop(0, count - 1, hop, so_far)


def combine_estimates(earlier, later):
    return (
        earlier[0] * later[2] + later[0],
        earlier[1] * later[2] + later[1],
        earlier[2] * later[2],
    )


def weighted_gram(beam_rows, row_weight):
    return jnp.dot((beam_rows * row_weight[:, None]).T, beam_rows, precision=lax.Precision.HIGHEST)


def local(samples, taps_weight, retain):
    row_count = samples.shape[0]
    elem_width = samples.shape[1]
    tap_count = taps_weight.shape[0]
    beam_count = taps_weight.shape[2]
    sample_history = shifted(samples[row_count - (tap_count - 1) :], "tm", 1)
    extended = jnp.concatenate([sample_history, samples], 0)
    windowed = jnp.concatenate(
        [
            extended[
                tap_count - 1 - filter_tap_index : tap_count - 1 - filter_tap_index + row_count
            ]
            for filter_tap_index in range(tap_count)
        ],
        1,
    )
    filters = taps_weight.reshape(tap_count * elem_width, beam_count)
    log_retain = jnp.log(retain)
    log_total = jnp.sum(log_retain)
    row_weight = jnp.exp(log_total - jnp.cumsum(log_retain))
    factor = jnp.exp(log_total)
    mass_aggregate = jnp.sum(row_weight)
    groups = lax.axis_size("elem")
    cluster_entry = lax.axis_index("elem")
    columns = beam_count // groups
    unit_matrix = jnp.eye(beam_count, dtype=jnp.float32)
    beam_rows = lax.psum(jnp.dot(windowed, filters, preferred_element_type=jnp.float32), "elem")
    gram_block = weighted_gram(beam_rows, row_weight)
    empty = (jnp.zeros_like(gram_block), jnp.zeros((), jnp.float32), jnp.ones((), jnp.float32))
    prefix = entering((gram_block, mass_aggregate, factor), "tm", combine_estimates, empty)
    gram_sum, count_sum, unused = combine_estimates(prefix, (gram_block, mass_aggregate, factor))
    covariance_estimate = gram_sum / count_sum + loading_level * unit_matrix
    lower_factor = jnp.linalg.cholesky(covariance_estimate)
    inverse_lower = jax.scipy.linalg.solve_triangular(lower_factor, unit_matrix, lower=True)
    local_rows = lax.dynamic_slice_in_dim(inverse_lower, cluster_entry * columns, columns, 0)
    return lax.dot_general(
        local_rows, beam_rows, (((1,), (1,)), ((), ())), precision=lax.Precision.HIGHEST
    )


def solution(mesh):
    placed = (P("tm", "elem"), P(None, "elem", None), P("tm"))
    return jax.shard_map(
        local, mesh=mesh, in_specs=placed, out_specs=P("elem", "tm"), check_vma=False
    )
```

profile of v0, /device:TPU:1, one launch (start us, length us, event | category | flops | bytes accessed | tf_op | source)
XLA Modules:
  0.0 556.6 jit_solution(1617515024383423267)
XLA Ops:
  7.3 4.8 collective-permute-start
  21.7 4.6 fusion.74
  28.7 76.0 %all-reduce.6.cloned.1.call-done = f32[768,512]{1,0:T(8,128)} async-done(((f32[768,512]{1,0:T(8,128)}), f32[768,512]{1,0:T(8,128)}) %all-reduce.6.cloned.1.call-update) | async-done | bytes 1572880 | tf_op jit(solution)/shard_map/psum | solution.py:67
  104.7 5.8 %fusion.1 = f32[512,512]{1,0:T(8,128)} fusion(f32[768,512]{1,0:T(8,128)} %all-reduce.6.cloned.1.call-done, f32[768]{0:T(1024)S(1)} %get-tuple-element.205), kind=kOutput, calls=%fused_computation.4 | convolution fusion | flops 2416312320 | bytes 2624512 | tf_op jit(solution)/shard_map/dot_general | solution.py:38
  113.8 67.2 %all-reduce.3 = (f32[32]{0:T(128)S(1)}, f32[32]{0:T(128)S(1)}) all-reduce(f32[32]{0:T(128)S(1)} %dynamic-update-slice.23, f32[32]{0:T(128)S(1)} %dynamic-update-slice.24), channel_id=1, replica_groups=mesh['elem'=8,'tm'=32] {'tm'}, use_global_device_ids=true, to_apply=%add.1 | all-reduce | flops 64 | bytes 512
  184.5 48.6 %all-gather.3.cloned.1.call-done = f32[16384,512]{1,0:T(8,128)} async-done(((f32[512,512]{1,0:T(8,128)}), f32[16384,512]{1,0:T(8,128)}) %all-gather.3.cloned.1.call-update) | async-done | bytes 33554448 | tf_op jit(solution)/shard_map/all_gather | solution.py:17
  233.0 161.5 %while.18 = (s32[]{:T(128)}, f32[512,512]{1,0:T(8,128)S(1)}, f32[]{:T(128)}, s32[]{:T(128)}, f32[32]{0:T(128)S(1)}, /*index=5*/f32[32,512,512]{2,1,0:T(8,128)}, f32[32]{0:T(128)S(1)}, s32[]{:T(128)}, s32[]{:T(128)}) while((s32[]{:T(128)}, f32[512,512]{1,0:T(8,128)S(1)}, f32[]{:T(128)}, s32[]{:T(128)}, f32[32]{0:T(128)S(1)}, ...), condition=%wide.region_6.7_spmd.clone, body=%wide.region_5.6_spmd.clone.sunk | while | flops 1048583 | bytes 3145910 | solution.py:26
  233.7 2.4 fusion.87
  238.9 2.4 fusion.87
  280.4 2.4 fusion.87
  290.8 2.4 fusion.87
  301.2 2.4 fusion.87
  379.1 2.4 fusion.87
  389.5 2.4 fusion.87
  396.3 11.7 %cholesky.103 = f32[128,128]{1,0:T(8,128)S(1)} custom-call(f32[128,128]{1,0:T(8,128)S(1)} %cholesky.263), custom_call_target="Cholesky" | custom-call | tf_op jit(solution)/shard_map/jit(cholesky)/cholesky | solution.py:73
  408.1 9.8 %custom-call.31 = f32[1,128,128]{1,2,0:T(8,128)S(1)} custom-call(f32[1,128,128]{2,1,0:T(8,128)S(1)} %get-tuple-element.203), custom_call_target="InvertDiagBlocksLowerTriangular" | custom-call | tf_op jit(solution)/shard_map/jit(cholesky)/cholesky | solution.py:73
  418.5 11.7 %cholesky.215 = f32[128,128]{1,0:T(8,128)S(1)} custom-call(f32[128,128]{1,0:T(8,128)S(1)} %cholesky.267), custom_call_target="Cholesky" | custom-call | tf_op jit(solution)/shard_map/jit(cholesky)/cholesky | solution.py:73
  430.6 10.0 %custom-call.32 = f32[1,128,128]{1,2,0:T(8,128)S(1)} custom-call(f32[1,128,128]{2,1,0:T(8,128)S(1)} %get-tuple-element.201), custom_call_target="InvertDiagBlocksLowerTriangular" | custom-call | tf_op jit(solution)/shard_map/jit(cholesky)/cholesky | solution.py:73
  442.7 11.7 %cholesky.236 = f32[128,128]{1,0:T(8,128)S(1)} custom-call(f32[128,128]{1,0:T(8,128)S(1)} %cholesky.272), custom_call_target="Cholesky" | custom-call | tf_op jit(solution)/shard_map/jit(cholesky)/cholesky | solution.py:73
  454.6 9.8 %custom-call.33 = f32[1,128,128]{1,2,0:T(8,128)S(1)} custom-call(f32[1,128,128]{2,1,0:T(8,128)S(1)} %get-tuple-element.199), custom_call_target="InvertDiagBlocksLowerTriangular" | custom-call | tf_op jit(solution)/shard_map/jit(cholesky)/cholesky | solution.py:73
  466.0 11.9 %cholesky.253 = f32[128,128]{1,0:T(8,128)S(1)} custom-call(f32[128,128]{1,0:T(8,128)S(1)} %convolution_subtract_fusion.5), custom_call_target="Cholesky" | custom-call | tf_op jit(solution)/shard_map/jit(cholesky)/cholesky | solution.py:73
  483.8 14.9 %while.17 = (s32[]{:T(128)}, f32[512,512]{0,1:T(8,128)}, s32[4,2]{0,1:T(2,128)S(1)}, f32[4,128,128]{2,1,0:T(8,128)}, s32[]{:T(128)}) while((s32[]{:T(128)}, f32[512,512]{0,1:T(8,128)}, s32[4,2]{0,1:T(2,128)S(1)}, f32[4,128,128]{2,1,0:T(8,128)}, s32[]{:T(128)}) %tuple.57), condition=%wide.while_cond, body=%wide.while_body.sunk | while | flops 2 | bytes 393829 | solution.py:74
  498.7 40.1 %custom-call.34 = f32[4,128,128]{1,2,0:T(8,128)S(1)} custom-call(f32[4,128,128]{2,1,0:T(8,128)} %get-tuple-element.139), custom_call_target="InvertDiagBlocksLowerTriangular" | custom-call | tf_op jit(solution)/shard_map/jit(_solve_triangular)/triangular_solve | solution.py:74
  544.4 2.5 convolution_subtract_fusion.2
  (196 shorter events, 151.0 us)
Async XLA Ops:
  6.5 14.3 %copy-start = (bf16[768,256]{1,0:T(8,128)(2,1)S(1)}, bf16[768,256]{1,0:T(8,128)(2,1)}, u32[]{:S(2)}) copy-start(bf16[768,256]{1,0:T(8,128)(2,1)} %param.5) | copy-start | bytes 1179652
  6.5 98.2 %all-reduce.6.cloned.1.call-start = ((), (), s32[]{:S(2)}) async-start(), calls=%async_computation | async-start | bytes 3145728 | tf_op jit(solution)/shard_map/psum | solution.py:67
  7.3 14.3 %copy-start.4 = (bf16[16,256,512]{2,1,0:T(8,128)(2,1)S(1)}, bf16[16,256,512]{2,1,0:T(8,128)(2,1)}, u32[]{:S(2)}) copy-start(bf16[16,256,512]{2,1,0:T(8,128)(2,1)} %param.6) | copy-start | bytes 12582916
  7.3 5.8 %collective-permute-start = (bf16[15,256]{1,0:T(8,128)(2,1)S(1)}, bf16[15,256]{1,0:T(8,128)(2,1)S(1)}, u32[]{:S(2)}, u32[]{:S(2)}) collective-permute-start(bf16[15,256]{1,0:T(8,128)(2,1)S(1)} %slice.169), channel_id=1, source_target_pairs={{0,1},{1,2},{2,3},{3,4},{4,5},{5,6},{6,7},{7,8},{8,9},{9,10},{10,1... | collective-permute-start | bytes 23048 | tf_op jit(solution)/shard_map/ppermute | solution.py:12
  21.6 4.7 copy-start.3
  26.2 85.0 %copy-start.5 = (u32[256]{0:T(256)S(1)}, u32[256]{0:T(256)}, u32[]{:S(2)}) copy-start(u32[256]{0:T(256)} %constant.208) | copy-start | bytes 3076
  26.2 206.8 %all-gather.3.cloned.1.call-start = ((), (), s32[]{:S(2)}) async-start(), calls=%async_computation.1 | async-start | bytes 34603008 | tf_op jit(solution)/shard_map/all_gather | solution.py:17
  396.3 34.3 %copy-start.2 = (f32[512,512]{1,0:T(8,128)}, f32[512,512]{1,0:T(8,128)S(1)}, u32[]{:S(2)}) copy-start(f32[512,512]{1,0:T(8,128)S(1)} %fusion.3) | copy-start | bytes 3145732
  440.7 106.6 %copy-start.1 = (f32[768,512]{1,0:T(8,128)S(1)}, f32[768,512]{1,0:T(8,128)}, u32[]{:S(2)}) copy-start(f32[768,512]{1,0:T(8,128)} %all-reduce.6.cloned.1.call-done) | copy-start | bytes 4718596
Sparse Core Ops, SparseCore 0:
  26.4 78.2 all-reduce.5
  110.6 122.3 all-gather.2
where the time goes:
time: 566 us; the launch traced here: 557 us
  other arithmetic  209 us (37%)
  waiting for transfers between devices  125 us (22%)
  blocking collectives  67.2 us (12%)
  local copies, waits for them, and re-layouts  63.6 us (11%)
  loops' own time  44.4 us (8%)
  matrix products  25.2 us (4%)
  between operations  18 us (3%)
    another operation x14, other arithmetic, local(): lower_factor = jnp.linalg.cholesky(covariance_estimate)  78.8 us
    psum x1, waiting for transfers between devices, local(): lax.psum(jnp.dot(windowed, filters, preferred_element_type=jnp.float32),...  76 us
    select_n x31, other arithmetic, hop(): jnp.where(position < mine, new, old)  75.8 us
    unnamed x1, blocking collectives  67.2 us
    all_gather x1, waiting for transfers between devices, entering(): pieces = jax.tree.map(lambda part: lax.all_gather(part, axis), value)  48.6 us
    another operation x1, loops' own time, entering(): return lax.fori_loop(0, count - 1, hop, so_far)  44.4 us
    dynamic_slice x62, local copies, waits for them, and re-layouts, hop(): longer = join(so_far, jax.tree.map(lambda part: part[position], pieces))  41.3 us
    another operation x3, other arithmetic, local(): jax.scipy.linalg.solve_triangular(lower_factor, unit_matrix, lower=True)  41.2 us
  transfers between devices with their start and end apart: 3, of which 2 were waited for; matrix products, arithmetic and copies ran while one was open for 2% of the time, Pallas kernels for 0%

commit v1 on v0

--- a/solution.py
+++ b/solution.py
@@ -2,6 +2,7 @@
 import jax.numpy as jnp
 from jax import lax
 from jax.sharding import PartitionSpec as P
+from jax.lax import all_gather
 
 loading_level = 0.1
 
@@ -64,7 +65,8 @@
     cluster_entry = lax.axis_index("elem")
     columns = beam_count // groups
     unit_matrix = jnp.eye(beam_count, dtype=jnp.float32)
-    beam_rows = lax.psum(jnp.dot(windowed, filters, preferred_element_type=jnp.float32), "elem")
+    my_data = jnp.dot(windowed, filters, preferred_element_type=jnp.float32)
+    beam_rows = all_gather(my_data, "elem").sum(axis=0)
     gram_block = weighted_gram(beam_rows, row_weight)
     empty = (jnp.zeros_like(gram_block), jnp.zeros((), jnp.float32), jnp.ones((), jnp.float32))
     prefix = entering((gram_block, mass_aggregate, factor), "tm", combine_estimates, empty)

time: 566 us -> 617 us (1.090)
  waiting for transfers between devices: 125 us -> 182 us
  loops' own time: 44.4 us -> 37.1 us
    all_gather x0 -> x1, waiting for transfers between devices: none -> 134 us  [local(): beam_rows = all_gather(my_data, 'elem').sum(axis=0)]
    psum x1 -> x0, waiting for transfers between devices: 76 us -> none  [local(): lax.psum(jnp.dot(windowed, filters, preferred_element_type=jnp.float32),...]
    another operation x1, loops' own time: 44.4 us -> 37.1 us  [entering(): return lax.fori_loop(0, count - 1, hop, so_far)]
    reduce_sum x0 -> x1, other arithmetic: none -> 6.32 us  [local(): beam_rows = all_gather(my_data, 'elem').sum(axis=0)]
where the time goes in v1:
time: 617 us; the launch traced here: 606 us
  other arithmetic  214 us (35%)
  waiting for transfers between devices  182 us (29%)
  blocking collectives  63.7 us (10%)
  local copies, waits for them, and re-layouts  62.9 us (10%)
  loops' own time  37.1 us (6%)
  matrix products  24.3 us (4%)
  between operations  17.9 us (3%)
    all_gather x1, waiting for transfers between devices, local(): beam_rows = all_gather(my_data, 'elem').sum(axis=0)  134 us
    another operation x14, other arithmetic, local(): lower_factor = jnp.linalg.cholesky(covariance_estimate)  78.7 us
    select_n x31, other arithmetic, hop(): jnp.where(position < mine, new, old)  72.2 us
    unnamed x1, blocking collectives  63.7 us
    all_gather x1, waiting for transfers between devices, entering(): pieces = jax.tree.map(lambda part: lax.all_gather(part, axis), value)  47.4 us
    another operation x3, other arithmetic, local(): jax.scipy.linalg.solve_triangular(lower_factor, unit_matrix, lower=True)  41.2 us
    another operation x1, loops' own time, entering(): return lax.fori_loop(0, count - 1, hop, so_far)  37.1 us
    dynamic_slice x62, local copies, waits for them, and re-layouts, hop(): longer = join(so_far, jax.tree.map(lambda part: part[position], pieces))  36.8 us
  transfers between devices with their start and end apart: 3, of which 2 were waited for; matrix products, arithmetic and copies ran while one was open for 2% of the time, Pallas kernels for 0%

profile of v1, /device:TPU:1, one launch (start us, length us, event | category | flops | bytes accessed | tf_op | source)
XLA Modules:
  0.0 605.9 jit_solution(7416201626087092520)
XLA Ops:
  7.3 4.8 collective-permute-start
  21.7 4.6 fusion.74
  28.8 134.2 %all-gather.5.cloned.1.call-done = f32[6144,512]{1,0:T(8,128)} async-done(((f32[768,512]{1,0:T(8,128)}), f32[6144,512]{1,0:T(8,128)}) %all-gather.5.cloned.1.call-update) | async-done | bytes 12582928 | tf_op jit(solution)/shard_map/all_gather | solution.py:69
  163.1 6.3 %reduce_sum.28 = f32[768,512]{1,0:T(8,128)S(1)} reduce(f32[8,768,512]{2,1,0:T(8,128)} %bitcast.72, f32[]{:T(128)} %copy.76), dimensions={0}, to_apply=%region_0.0 | reduce | flops 2752512 | bytes 14155780 | tf_op jit(solution)/shard_map/reduce_sum | solution.py:69
  169.4 3.9 fusion.1
  176.9 63.7 %all-reduce.3 = (f32[32]{0:T(128)S(1)}, f32[32]{0:T(128)S(1)}) all-reduce(f32[32]{0:T(128)S(1)} %dynamic-update-slice.23, f32[32]{0:T(128)S(1)} %dynamic-update-slice.24), channel_id=1, replica_groups=mesh['elem'=8,'tm'=32] {'tm'}, use_global_device_ids=true, to_apply=%add.1 | all-reduce | flops 64 | bytes 512
  241.7 2.6 copy.16
  244.3 47.4 %all-gather.7.cloned.1.call-done = f32[16384,512]{1,0:T(8,128)} async-done(((f32[512,512]{1,0:T(8,128)}), f32[16384,512]{1,0:T(8,128)}) %all-gather.7.cloned.1.call-update) | async-done | bytes 33554448 | tf_op jit(solution)/shard_map/all_gather | solution.py:18
  291.7 146.0 %while.18 = (s32[]{:T(128)}, f32[512,512]{1,0:T(8,128)S(1)}, f32[]{:T(128)}, s32[]{:T(128)}, f32[32]{0:T(128)S(1)}, /*index=5*/f32[32,512,512]{2,1,0:T(8,128)}, f32[32]{0:T(128)S(1)}, s32[]{:T(128)}, s32[]{:T(128)}) while((s32[]{:T(128)}, f32[512,512]{1,0:T(8,128)S(1)}, f32[]{:T(128)}, s32[]{:T(128)}, f32[32]{0:T(128)S(1)}, ...), condition=%wide.region_6.7_spmd.clone, body=%wide.region_5.6_spmd.clone.sunk | while | flops 1048583 | bytes 3145910 | solution.py:27
  292.2 2.3 fusion.87
  296.9 2.3 fusion.87
  301.6 2.3 fusion.87
  320.4 2.3 fusion.87
  325.1 2.3 fusion.87
  445.2 11.7 %cholesky.103 = f32[128,128]{1,0:T(8,128)S(1)} custom-call(f32[128,128]{1,0:T(8,128)S(1)} %cholesky.263), custom_call_target="Cholesky" | custom-call | tf_op jit(solution)/shard_map/jit(cholesky)/cholesky | solution.py:75
  457.0 9.8 %custom-call.31 = f32[1,128,128]{1,2,0:T(8,128)S(1)} custom-call(f32[1,128,128]{2,1,0:T(8,128)S(1)} %get-tuple-element.203), custom_call_target="InvertDiagBlocksLowerTriangular" | custom-call | tf_op jit(solution)/shard_map/jit(cholesky)/cholesky | solution.py:75
  469.3 11.7 %cholesky.215 = f32[128,128]{1,0:T(8,128)S(1)} custom-call(f32[128,128]{1,0:T(8,128)S(1)} %cholesky.267), custom_call_target="Cholesky" | custom-call | tf_op jit(solution)/shard_map/jit(cholesky)/cholesky | solution.py:75
  481.4 10.0 %custom-call.32 = f32[1,128,128]{1,2,0:T(8,128)S(1)} custom-call(f32[1,128,128]{2,1,0:T(8,128)S(1)} %get-tuple-element.201), custom_call_target="InvertDiagBlocksLowerTriangular" | custom-call | tf_op jit(solution)/shard_map/jit(cholesky)/cholesky | solution.py:75
  493.4 11.7 %cholesky.236 = f32[128,128]{1,0:T(8,128)S(1)} custom-call(f32[128,128]{1,0:T(8,128)S(1)} %cholesky.272), custom_call_target="Cholesky" | custom-call | tf_op jit(solution)/shard_map/jit(cholesky)/cholesky | solution.py:75
  505.2 9.8 %custom-call.33 = f32[1,128,128]{1,2,0:T(8,128)S(1)} custom-call(f32[1,128,128]{2,1,0:T(8,128)S(1)} %get-tuple-element.199), custom_call_target="InvertDiagBlocksLowerTriangular" | custom-call | tf_op jit(solution)/shard_map/jit(cholesky)/cholesky | solution.py:75
  516.7 11.9 %cholesky.253 = f32[128,128]{1,0:T(8,128)S(1)} custom-call(f32[128,128]{1,0:T(8,128)S(1)} %convolution_subtract_fusion.5), custom_call_target="Cholesky" | custom-call | tf_op jit(solution)/shard_map/jit(cholesky)/cholesky | solution.py:75
  534.3 14.4 %while.17 = (s32[]{:T(128)}, f32[512,512]{0,1:T(8,128)}, s32[4,2]{0,1:T(2,128)S(1)}, f32[4,128,128]{2,1,0:T(8,128)}, s32[]{:T(128)}) while((s32[]{:T(128)}, f32[512,512]{0,1:T(8,128)}, s32[4,2]{0,1:T(2,128)S(1)}, f32[4,128,128]{2,1,0:T(8,128)}, s32[]{:T(128)}) %tuple.57), condition=%wide.while_cond, body=%wide.while_body.sunk | while | flops 2 | bytes 393829 | solution.py:76
  548.7 40.1 %custom-call.34 = f32[4,128,128]{1,2,0:T(8,128)S(1)} custom-call(f32[4,128,128]{2,1,0:T(8,128)} %get-tuple-element.139), custom_call_target="InvertDiagBlocksLowerTriangular" | custom-call | tf_op jit(solution)/shard_map/jit(_solve_triangular)/triangular_solve | solution.py:76
  593.6 2.5 convolution_subtract_fusion.2
  (195 shorter events, 152.6 us)
Async XLA Ops:
  6.5 14.3 %copy-start = (bf16[768,256]{1,0:T(8,128)(2,1)S(1)}, bf16[768,256]{1,0:T(8,128)(2,1)}, u32[]{:S(2)}) copy-start(bf16[768,256]{1,0:T(8,128)(2,1)} %param.5) | copy-start | bytes 1179652
  6.5 156.5 %all-gather.5.cloned.1.call-start = ((), (), s32[]{:S(2)}) async-start(), calls=%async_computation | async-start | bytes 14155776 | tf_op jit(solution)/shard_map/all_gather | solution.py:69
  7.3 14.3 %copy-start.3 = (bf16[16,256,512]{2,1,0:T(8,128)(2,1)S(1)}, bf16[16,256,512]{2,1,0:T(8,128)(2,1)}, u32[]{:S(2)}) copy-start(bf16[16,256,512]{2,1,0:T(8,128)(2,1)} %param.6) | copy-start | bytes 12582916
  7.3 5.8 collective-permute-start
  21.6 4.7 copy-start.2
  26.3 265.4 %all-gather.7.cloned.1.call-start = ((), (), s32[]{:S(2)}) async-start(), calls=%async_computation.1 | async-start | bytes 34603008 | tf_op jit(solution)/shard_map/all_gather | solution.py:18
  163.1 11.0 %copy-start.4 = (u32[256]{0:T(256)S(1)}, u32[256]{0:T(256)}, u32[]{:S(2)}) copy-start(u32[256]{0:T(256)} %constant.208) | copy-start | bytes 3076
  444.2 1.0 copy-start.1
Sparse Core Ops, SparseCore 0:
  26.4 136.6 all-gather.4
  173.4 118.1 all-gather.6
